TPU v7x, 128 devices: a whole 4x4x4 slice. The times are simulated.
128 devices in a mesh: row: 8 (over x, y_lo), col: 16 (over z, y_hi, core).
Axes of the slice: x: 4, y: 4 (y_hi: 2, y_lo: 2; y = y_hi * 2 + y_lo), z: 4, core: 2. Of those that a mesh axis runs over, the one named last changes fastest.
Arguments:
- atom_blocks: float32 [128, 16, 128, 128], P('row', 'col'), may hold values from -6 to 6
- grid_position: int32 [128], replicated, may hold values from 0 to 127, as said below
- pattern: int32 [128, 16], replicated, may hold values from -1 to 127, as said below
Outputs:
- square: float32 [128, 16, 128, 128], P('row', 'col')
- update: float32 [128, 16, 128, 128], P('row', 'col')
Inputs may be any that keep to these rules, and one draw needn't show every extreme that they name: grid_position is a permutation; the 16 atom block rows a with a // 16 equal put at most 2 grid positions into any one run of 16 grid positions that starts at a multiple of 16, and exactly 2 into some run. `pattern`: each row holds 12 different block columns, one of them its own index, and -1 in its other slots; all slots s that hold one block column j have the same s; the block rows lie on a cycle of 128 places, not given, on which each row's columns lie within 16 places in a row around its own.
All inputs are finite; a program needn't handle non-finite values.
Results may differ from a plain program's by a relative error of at most 0.0003.
Values sent between devices are 32-bit elements; how exact they have to be, the bound alone decides.
No kernel may reach another device: no remote copies, remote signals or barrier semaphores. Data moves between devices by JAX's collectives and lax.ppermute only.
A program may use at most 128 MiB of HBM per device.

v0:
```python
import math
import jax
import jax.numpy as jnp
from jax import lax
from jax.sharding import PartitionSpec as P

NZ = 12
HIGHEST = lax.Precision.HIGHEST


def atoms_of_rows(grid_position, grid_rows):
    atom_numbers = jnp.arange(grid_position.shape[0], dtype=jnp.int32)
    hits = grid_position[None, :] == grid_rows[:, None]
    return jnp.sum(jnp.where(hits, atom_numbers[None, :], 0), axis=1)


def on_device(atom_blocks, grid_position, pattern):
    group_rows = atom_blocks.shape[0]
    local_slots = atom_blocks.shape[1]
    block_edge = atom_blocks.shape[2]
    row_count = lax.axis_size("row")
    row_index = lax.axis_index("row")
    column_index = lax.axis_index("col")
    local_rows = jnp.arange(group_rows, dtype=jnp.int32)
    grid_rows = row_index * group_rows + local_rows
    grid_atoms = atoms_of_rows(grid_position, grid_rows)
    capacity = 2 * ((group_rows + 2 * row_count - 1) // (2 * row_count))
    local_place = lax.dynamic_slice_in_dim(grid_position, row_index * group_rows, group_rows)
    target = local_place // group_rows
    ranking = jnp.sum(
        (target[None, :] == target[:, None]) & (local_rows[None, :] < local_rows[:, None]), axis=1
    )
    slot_code = target * capacity + ranking
    flat_slots = jnp.arange(row_count * capacity, dtype=jnp.int32)
    source = jnp.sum(
        jnp.where(slot_code[None, :] == flat_slots[:, None], local_rows[None, :], 0), axis=1
    )
    outgoing = jnp.take(atom_blocks, source, axis=0).reshape(
        row_count, capacity, local_slots, block_edge, block_edge
    )
    incoming = lax.all_to_all(outgoing, "row", split_axis=0, concat_axis=0, tiled=True)
    source_group = grid_atoms // group_rows
    within = grid_atoms % group_rows
    group_targets = (grid_position // group_rows).reshape(row_count, group_rows)
    their_targets = jnp.take(group_targets, source_group, axis=0)
    arrival = jnp.sum(
        (their_targets == row_index) & (local_rows[None, :] < within[:, None]), axis=1
    )
    slot_index = source_group * capacity + arrival
    arrived = incoming.reshape(row_count * capacity, local_slots, block_edge, block_edge)
    grid_blocks = jnp.take(arrived, slot_index, axis=0)
    grid_pattern = jnp.take(pattern, grid_atoms, axis=0)
    own_pattern = lax.dynamic_slice_in_dim(grid_pattern, column_index * local_slots, local_slots, 1)
    own_filled = own_pattern >= 0
    column_pattern = lax.dynamic_slice_in_dim(pattern, column_index * local_slots, local_slots, 1)
    start_scale = 1.0 / math.sqrt(NZ * block_edge)
    scale_back = math.sqrt(NZ * block_edge)
    matrix = jnp.where(own_filled[:, :, None, None], grid_blocks * start_scale, 0.0)

    def contribution(panel_part, right_panel):
        neighbours = jnp.maximum(grid_pattern, 0)
        right_rows = jnp.take(right_panel, jnp.take(grid_position, neighbours), axis=0)
        right_pattern = jnp.take(column_pattern, neighbours, axis=0)
        matches = (
            (right_pattern[:, :, :, None] == own_pattern[:, None, None, :])
            & own_filled[:, None, None, :]
            & (grid_pattern >= 0)[:, :, None, None]
        )
        weights = jnp.where(matches[:, :, 0, :, None, None], right_rows[:, :, 0][:, :, None], 0.0)
        return jnp.einsum("iupq,iutqr->itpr", panel_part, weights, precision=HIGHEST)

    def multiply(right_panel):
        return contribution(lax.all_gather(matrix, "col", axis=1, tiled=True), right_panel)

    right_panel = lax.all_gather(matrix, "row", axis=0, tiled=True)
    masked_square = multiply(right_panel)
    square_panel = lax.all_gather(masked_square, "row", axis=0, tiled=True)
    cubic = multiply(square_panel)
    square = masked_square * scale_back
    update = (1.5 * matrix - 0.5 * cubic) * scale_back
    return (square, update)


def solution(mesh):
    in_specs = (P("row", "col", None, None), P(), P())
    out_specs = (P("row", "col", None, None), P("row", "col", None, None))
    return jax.shard_map(
        on_device, mesh=mesh, in_specs=in_specs, out_specs=out_specs, check_vma=False
    )
```

profile of v0, /device:TPU:5, one launch (start us, length us, event | category | flops | bytes accessed | tf_op | source)
XLA Modules:
  0.0 577.1 jit_solution(7751069718583219607)
XLA Ops:
  7.2 0.0 copy-start
  7.2 0.0 copy-start.2
  7.2 0.9 select_reduce_fusion.1
  8.1 0.7 and_select_fusion.3
  8.9 0.2 convert_reduce_fusion.1
  9.1 0.7 multiply_add_fusion
  9.8 0.1 select_reduce_fusion
  10.0 0.0 copy-done
  10.0 0.6 gather_fusion.3
  10.6 1.1 bitcast_select_fusion.1
  11.7 5.3 all-to-all-start
  17.0 0.0 all-gather.4.cloned.1.call-start
  17.0 0.7 and_select_fusion.1
  17.6 0.1 reshape.251
  17.7 0.1 copy.38
  17.8 0.8 copy.41
  18.6 0.1 fusion.32
  18.7 0.6 gather_fusion.1
  19.3 0.6 gather_fusion
  19.8 0.1 broadcast_maximum_fusion
  19.9 0.2 compare_reduce_fusion
  20.1 0.2 convert_reduce_fusion
  20.3 10.3 %all-to-all-done = f32[8,2,1,128,128]{4,3,1,2,0:T(8,128)S(1)} async-done(((f32[8,2,1,128,128]{4,3,1,2,0:T(8,128)}), f32[8,2,1,128,128]{4,3,1,2,0:T(8,128)S(1)}, u32[]{:S(2)}, u32[]{:S(2)}) %all-to-all-start) | async-done | bytes 1048608 | tf_op jit(solution)/shard_map/all_to_all | solution.py:41
  30.7 0.6 gather_fusion.4
  31.3 1.2 fusion.31
  32.5 0.0 all-gather.4.cloned.1.call-update
  32.5 0.0 all-gather.6.cloned.1.call-start
  32.6 0.7 all-gather.6.cloned.1.call-update
  33.3 0.0 all-gather.8.cloned.1.call-start
  33.3 0.1 reshape.343
  33.4 1.9 gather_fusion.5
  35.3 0.7 dynamic-slice_bitcast_fusion
  36.0 1.9 gather_fusion.2
  37.9 0.1 reshape.357
  37.9 0.1 gather.48
  38.0 0.2 dynamic-slice_reduce_fusion
  38.2 0.1 compare_and_fusion
  38.3 0.1 reshape.359
  38.4 169.3 %all-gather.4.cloned.1.call-done = f32[128,1,128,128]{3,2,1,0:T(8,128)} async-done(((f32[16,1,128,128]{3,2,1,0:T(8,128)}), f32[128,1,128,128]{3,2,1,0:T(8,128)}) %all-gather.4.cloned.1.call-update) | async-done | bytes 8388624 | tf_op jit(solution)/shard_map/all_gather | solution.py:75
  207.7 15.6 %gather_fusion.6 = f32[256,128,128]{2,1,0:T(8,128)} fusion(f32[128,128,128]{2,1,0:T(8,128)} %bitcast.69, s32[1024]{0:T(1024)S(1)} %pad_clamp_fusion), kind=kCustom, calls=%fused_computation.3.clone | custom fusion | bytes 33555456 | tf_op jit(solution)/shard_map/jit(_take)/gather | solution.py:62
  223.2 18.0 %copy.45 = f32[16,16,1,128,128]{3,4,1,0,2:T(8,128)} copy(f32[16,16,1,128,128]{4,3,1,0,2:T(8,128)} %bitcast.68) | data formatting | bytes 33554432 | tf_op jit(solution)/shard_map/jit(_take)/gather | solution.py:62
  241.2 80.1 %all-gather.6.cloned.1.call-done = f32[16,16,128,128]{3,2,1,0:T(8,128)} async-done(((f32[16,1,128,128]{3,2,1,0:T(8,128)}), f32[16,16,128,128]{3,2,1,0:T(8,128)}) %all-gather.6.cloned.1.call-update) | async-done | bytes 16777232 | tf_op jit(solution)/shard_map/all_gather | solution.py:73
  321.4 23.0 %broadcast_multiply_fusion = (f32[16,1,128,128]{3,2,1,0:T(8,128)}, f32[16,1,128,128]{3,2,1,0:T(8,128)}) fusion(f32[16,16,128,128]{3,2,1,0:T(8,128)} %all-gather.6.cloned.1.call-done, f32[16,16,1,128,128]{3,4,1,0,2:T(8,128)} %copy.45, pred[16,16]{1,0:T(8,128)(4,1)S(1)} %get-tuple-element.8, pred[16,16]{1,0:T(8,128)(4,1)S(1)} %get-tuple-element.16), kind=kOutput, calls=%fused_computation.32 | convolution fusion | flops 6451101696 | bytes 35652096 | tf_op jit(solution)/shard_map/iupq,iutqr->itpr/dot_general | solution.py:70
  344.4 0.0 all-gather.8.cloned.1.call-update
  344.4 170.2 %all-gather.8.cloned.1.call-done = f32[128,1,128,128]{3,2,1,0:T(8,128)} async-done(((f32[16,1,128,128]{3,2,1,0:T(8,128)}), f32[128,1,128,128]{3,2,1,0:T(8,128)}) %all-gather.8.cloned.1.call-update) | async-done | bytes 8388624 | tf_op jit(solution)/shard_map/all_gather | solution.py:77
  514.6 15.4 %gather_fusion.7 = f32[256,128,128]{2,1,0:T(8,128)} fusion(f32[128,128,128]{2,1,0:T(8,128)} %bitcast.70, s32[1024]{0:T(1024)S(1)} %pad_clamp_fusion), kind=kCustom, calls=%fused_computation.5.clone | custom fusion | bytes 33555456 | tf_op jit(solution)/shard_map/jit(_take)/gather | solution.py:62
  530.0 17.8 %copy.47 = f32[16,16,1,128,128]{3,4,1,0,2:T(8,128)} copy(f32[16,16,1,128,128]{4,3,1,0,2:T(8,128)} %bitcast.67) | data formatting | bytes 33554432 | tf_op jit(solution)/shard_map/jit(_take)/gather | solution.py:62
  547.8 22.8 %fusion.27 = f32[16,1,128,128]{3,2,1,0:T(8,128)} fusion(f32[16,16,128,128]{3,2,1,0:T(8,128)} %all-gather.6.cloned.1.call-done, f32[16,16,1,128,128]{3,4,1,0,2:T(8,128)} %copy.47, pred[16,16]{1,0:T(8,128)(4,1)S(1)} %get-tuple-element.8, pred[16,16]{1,0:T(8,128)(4,1)S(1)} %get-tuple-element.16, f32[16,1,128,128]{3,2,1,0:T(8,128)S(1)} %copy-done.3), kind=kOutput, calls=%fused_computation.27 | convolution fusion | flops 6451888128 | bytes 35652096 | tf_op jit(solution)/shard_map/iupq,iutqr->itpr/dot_general | solution.py:70
  (14 shorter events, 0.1 us)
Async XLA Ops:
  7.2 2.8 copy-start
  7.2 26.2 %copy-start.2 = (s32[128]{0:T(128)S(1)}, s32[128]{0:T(128)}, u32[]{:S(2)}) copy-start(s32[128]{0:T(128)} %param.12) | copy-start | bytes 1540
  11.7 19.0 %all-to-all-start = ((f32[8,2,1,128,128]{4,3,1,2,0:T(8,128)}), f32[8,2,1,128,128]{4,3,1,2,0:T(8,128)S(1)}, u32[]{:S(2)}, u32[]{:S(2)}) async-start(f32[8,2,1,128,128]{4,3,1,2,0:T(8,128)} %bitcast.5), calls=%async_computation | async-start | bytes 2097152 | tf_op jit(solution)/shard_map/all_to_all | solution.py:41
  17.0 190.7 %all-gather.4.cloned.1.call-start = ((), (), s32[]{:S(2)}) async-start(), calls=%async_computation.1 | async-start | bytes 9437184 | tf_op jit(solution)/shard_map/all_gather | solution.py:75
  32.5 288.8 %all-gather.6.cloned.1.call-start = ((), (), s32[]{:S(2)}) async-start(), calls=%async_computation.2 | async-start | bytes 17825792 | tf_op jit(solution)/shard_map/all_gather | solution.py:73
  33.3 481.4 %all-gather.8.cloned.1.call-start = ((), (), s32[]{:S(2)}) async-start(), calls=%async_computation.3 | async-start | bytes 9437184 | tf_op jit(solution)/shard_map/all_gather | solution.py:77
  530.0 17.8 %copy-start.3 = (f32[16,1,128,128]{3,2,1,0:T(8,128)S(1)}, f32[16,1,128,128]{3,2,1,0:T(8,128)}, u32[]{:S(2)}) copy-start(f32[16,1,128,128]{3,2,1,0:T(8,128)} %fusion.31) | copy-start | bytes 3145732
  530.0 40.6 %copy-start.1 = (f32[16,1,128,128]{3,2,1,0:T(8,128)S(1)}, f32[16,1,128,128]{3,2,1,0:T(8,128)}, u32[]{:S(2)}) copy-start(f32[16,1,128,128]{3,2,1,0:T(8,128)} %param.11) | copy-start | bytes 3145732
Sparse Core Ops, SparseCore 0:
  32.6 174.9 all-gather.3
  210.7 110.6 all-gather.5
  344.6 170.0 all-gather.7
where the time goes:
time: 578 us; the launch traced here: 577 us
  waiting for transfers between devices  431 us (75%)
  local copies, waits for them, and re-layouts  75 us (13%)
  matrix products  45.9 us (8%)
  between operations  13.9 us (2%)
  other arithmetic  6.41 us (1%)
    all_gather x1, waiting for transfers between devices, on_device(): square_panel = lax.all_gather(masked_square, 'row', axis=0, tiled=True)  170 us
    all_gather x1, waiting for transfers between devices, on_device(): right_panel = lax.all_gather(matrix, 'row', axis=0, tiled=True)  169 us
    all_gather x1, waiting for transfers between devices, multiply(): lax.all_gather(matrix, 'col', axis=1, tiled=True)  80.1 us
    gather x4, local copies, waits for them, and re-layouts, contribution(): jnp.take(right_panel, jnp.take(grid_position, neighbours), axis=0)  66.7 us
    dot_general x2, matrix products, contribution(): jnp.einsum('iupq,iutqr->itpr', panel_part, weights, precision=HIGHEST)  45.9 us
  transfers between devices with their start and end apart: 4, of which 4 were waited for; matrix products, arithmetic and copies ran while one was open for 7% of the time, Pallas kernels for 0%

commit v1 on v0

--- a/solution.py
+++ b/solution.py
@@ -74,7 +74,9 @@
 
     right_panel = lax.all_gather(matrix, "row", axis=0, tiled=True)
     masked_square = multiply(right_panel)
-    square_panel = lax.all_gather(masked_square, "row", axis=0, tiled=True)
+    square_panel = jnp.concatenate(
+        lax.all_to_all(jnp.stack([masked_square] * lax.axis_size("row")), "row", 0, 0), axis=0
+    )
     cubic = multiply(square_panel)
     square = masked_square * scale_back
     update = (1.5 * matrix - 0.5 * cubic) * scale_back

time: 578 us -> 507 us (0.88)
  waiting for transfers between devices: 431 us -> 260 us
  blocking collectives: 0 us -> 95.6 us
    all_gather x1 -> x0, waiting for transfers between devices: 170 us -> none  [on_device(): square_panel = lax.all_gather(masked_square, 'row', axis=0, tiled=True)]
    all_to_all x0 -> x1, blocking collectives: none -> 95.6 us  [on_device(): lax.all_to_all(jnp.stack([masked_square] * lax.axis_size('row')), 'row',...]
  transfers between devices with their start and end apart: 4 -> 3, of which waited for: 4 -> 3; matrix products, arithmetic and copies ran while one was open for 7% -> 8% of each run, Pallas kernels for 0% -> 0%
where the time goes in v1:
time: 507 us; the launch traced here: 503 us
  waiting for transfers between devices  260 us (51%)
  blocking collectives  95.6 us (19%)
  local copies, waits for them, and re-layouts  75.8 us (15%)
  matrix products  45.4 us (9%)
  between operations  14.2 us (3%)
  other arithmetic  6.41 us (1%)
  starting transfers between devices  5.3 us (1%)
    all_gather x1, waiting for transfers between devices, on_device(): right_panel = lax.all_gather(matrix, 'row', axis=0, tiled=True)  169 us
    all_to_all x1, blocking collectives, on_device(): lax.all_to_all(jnp.stack([masked_square] * lax.axis_size('row')), 'row',...  95.6 us
    all_gather x1, waiting for transfers between devices, multiply(): lax.all_gather(matrix, 'col', axis=1, tiled=True)  80.1 us
    gather x4, local copies, waits for them, and re-layouts, contribution(): jnp.take(right_panel, jnp.take(grid_position, neighbours), axis=0)  66.5 us
    dot_general x2, matrix products, contribution(): jnp.einsum('iupq,iutqr->itpr', panel_part, weights, precision=HIGHEST)  45.4 us
    all_to_all x1, waiting for transfers between devices, on_device(): lax.all_to_all(outgoing, 'row', split_axis=0, concat_axis=0, tiled=True)  10.3 us
  transfers between devices with their start and end apart: 3, of which 3 were waited for; matrix products, arithmetic and copies ran while one was open for 8% of the time, Pallas kernels for 0%

profile of v1, /device:TPU:5, one launch (start us, length us, event | category | flops | bytes accessed | tf_op | source)
XLA Modules:
  0.0 503.1 jit_solution(15175456770669681130)
XLA Ops:
  7.2 0.0 copy-start
  7.2 0.0 copy-start.2
  7.2 0.9 select_reduce_fusion.1
  8.1 0.7 and_select_fusion.3
  8.9 0.2 convert_reduce_fusion.1
  9.1 0.7 multiply_add_fusion
  9.8 0.1 select_reduce_fusion
  10.0 0.0 copy-done
  10.0 0.6 gather_fusion.3
  10.6 1.1 bitcast_select_fusion.1
  11.7 5.3 %all-to-all-start = ((f32[8,2,1,128,128]{4,3,1,2,0:T(8,128)}), f32[8,2,1,128,128]{4,3,1,2,0:T(8,128)S(1)}, u32[]{:S(2)}, u32[]{:S(2)}) async-start(f32[8,2,1,128,128]{4,3,1,2,0:T(8,128)} %bitcast.5), calls=%async_computation | async-start | bytes 2097152 | tf_op jit(solution)/shard_map/all_to_all | solution.py:41
  17.0 0.0 all-gather.3.cloned.1.call-start
  17.0 0.7 and_select_fusion.1
  17.6 0.1 reshape.257
  17.7 0.1 copy.37
  17.8 0.8 copy.40
  18.6 0.1 fusion.29
  18.7 0.6 gather_fusion.1
  19.3 0.6 gather_fusion
  19.8 0.1 broadcast_maximum_fusion
  19.9 0.2 compare_reduce_fusion
  20.1 0.2 convert_reduce_fusion
  20.3 10.3 %all-to-all-done = f32[8,2,1,128,128]{4,3,1,2,0:T(8,128)S(1)} async-done(((f32[8,2,1,128,128]{4,3,1,2,0:T(8,128)}), f32[8,2,1,128,128]{4,3,1,2,0:T(8,128)S(1)}, u32[]{:S(2)}, u32[]{:S(2)}) %all-to-all-start) | async-done | bytes 1048608 | tf_op jit(solution)/shard_map/all_to_all | solution.py:41
  30.7 0.6 gather_fusion.4
  31.3 1.2 fusion.28
  32.5 0.0 all-gather.3.cloned.1.call-update
  32.5 0.0 all-gather.5.cloned.1.call-start
  32.6 0.7 all-gather.5.cloned.1.call-update
  33.3 0.1 reshape.350
  33.4 0.0 copy-done.2
  33.4 1.9 gather_fusion.5
  35.2 0.7 dynamic-slice_bitcast_fusion
  35.9 1.9 gather_fusion.2
  37.8 0.1 reshape.364
  37.9 0.1 gather.48
  38.0 0.2 dynamic-slice_reduce_fusion
  38.2 0.1 compare_and_fusion
  38.2 0.1 reshape.366
  38.3 169.3 %all-gather.3.cloned.1.call-done = f32[128,1,128,128]{3,2,1,0:T(8,128)} async-done(((f32[16,1,128,128]{3,2,1,0:T(8,128)}), f32[128,1,128,128]{3,2,1,0:T(8,128)}) %all-gather.3.cloned.1.call-update) | async-done | bytes 8388624 | tf_op jit(solution)/shard_map/all_gather | solution.py:75
  207.7 15.6 %gather_fusion.6 = f32[256,128,128]{2,1,0:T(8,128)} fusion(f32[128,128,128]{2,1,0:T(8,128)} %bitcast.72, s32[1024]{0:T(1024)S(1)} %pad_clamp_fusion), kind=kCustom, calls=%fused_computation.3.clone | custom fusion | bytes 33555456 | tf_op jit(solution)/shard_map/jit(_take)/gather | solution.py:62
  223.2 18.0 %copy.44 = f32[16,16,1,128,128]{3,4,1,0,2:T(8,128)} copy(f32[16,16,1,128,128]{4,3,1,0,2:T(8,128)} %bitcast.71) | data formatting | bytes 33554432 | tf_op jit(solution)/shard_map/jit(_take)/gather | solution.py:62
  241.2 80.1 %all-gather.5.cloned.1.call-done = f32[16,16,128,128]{3,2,1,0:T(8,128)} async-done(((f32[16,1,128,128]{3,2,1,0:T(8,128)}), f32[16,16,128,128]{3,2,1,0:T(8,128)}) %all-gather.5.cloned.1.call-update) | async-done | bytes 16777232 | tf_op jit(solution)/shard_map/all_gather | solution.py:73
  321.3 22.7 %bitcast_multiply_fusion = (f32[16,1,128,128]{3,2,1,0:T(8,128)}, f32[16,128,128,1]{1,2,3,0:T(8,128)S(1)}) fusion(f32[16,16,128,128]{3,2,1,0:T(8,128)} %all-gather.5.cloned.1.call-done, f32[16,16,1,128,128]{3,4,1,0,2:T(8,128)} %copy.44, pred[16,16]{1,0:T(8,128)(4,1)S(1)} %get-tuple-element.8, pred[16,16]{1,0:T(8,128)(4,1)S(1)} %get-tuple-element.16), kind=kOutput, calls=%fused_computation.27 | convolution fusion | flops 6451101696 | bytes 35652096 | tf_op jit(solution)/shard_map/iupq,iutqr->itpr/dot_general | solution.py:70
  344.0 1.0 stack.2
  345.1 95.6 %all_to_all.10 = f32[8,16,1,128,128]{4,3,1,2,0:T(8,128)} all-to-all(f32[8,16,1,128,128]{4,3,1,2,0:T(8,128)S(1)} %stack.2), channel_id=1, replica_groups=mesh['row'=8,'col'=16] {'row'}, dimensions={0} | all-to-all | bytes 16777216 | tf_op jit(solution)/shard_map/all_to_all | solution.py:78
  440.6 15.2 %gather_fusion.7 = f32[256,128,128]{2,1,0:T(8,128)} fusion(f32[128,128,128]{2,1,0:T(8,128)} %bitcast.69, s32[1024]{0:T(1024)S(1)} %pad_clamp_fusion), kind=kCustom, calls=%fused_computation.5.clone | custom fusion | bytes 33555456 | tf_op jit(solution)/shard_map/jit(_take)/gather | solution.py:62
  455.8 17.8 %copy.46 = f32[16,16,1,128,128]{3,4,1,0,2:T(8,128)} copy(f32[16,16,1,128,128]{4,3,1,0,2:T(8,128)} %bitcast.70) | data formatting | bytes 33554432 | tf_op jit(solution)/shard_map/jit(_take)/gather | solution.py:62
  473.6 22.7 %fusion.24 = f32[16,1,128,128]{3,2,1,0:T(8,128)} fusion(f32[16,16,128,128]{3,2,1,0:T(8,128)} %all-gather.5.cloned.1.call-done, f32[16,16,1,128,128]{3,4,1,0,2:T(8,128)} %copy.46, pred[16,16]{1,0:T(8,128)(4,1)S(1)} %get-tuple-element.8, pred[16,16]{1,0:T(8,128)(4,1)S(1)} %get-tuple-element.16, f32[16,1,128,128]{3,2,1,0:T(8,128)S(1)} %copy-done.3), kind=kOutput, calls=%fused_computation.26 | convolution fusion | flops 6451888128 | bytes 35652096 | tf_op jit(solution)/shard_map/iupq,iutqr->itpr/dot_general | solution.py:70
  (13 shorter events, 0.1 us)
Async XLA Ops:
  7.2 2.8 copy-start
  7.2 26.2 %copy-start.2 = (s32[128]{0:T(128)S(1)}, s32[128]{0:T(128)}, u32[]{:S(2)}) copy-start(s32[128]{0:T(128)} %param.12) | copy-start | bytes 1540
  11.7 19.0 %all-to-all-start = ((f32[8,2,1,128,128]{4,3,1,2,0:T(8,128)}), f32[8,2,1,128,128]{4,3,1,2,0:T(8,128)S(1)}, u32[]{:S(2)}, u32[]{:S(2)}) async-start(f32[8,2,1,128,128]{4,3,1,2,0:T(8,128)} %bitcast.5), calls=%async_computation | async-start | bytes 2097152 | tf_op jit(solution)/shard_map/all_to_all | solution.py:41
  17.0 190.7 %all-gather.3.cloned.1.call-start = ((), (), s32[]{:S(2)}) async-start(), calls=%async_computation.2 | async-start | bytes 9437184 | tf_op jit(solution)/shard_map/all_gather | solution.py:75
  32.5 288.8 %all-gather.5.cloned.1.call-start = ((), (), s32[]{:S(2)}) async-start(), calls=%async_computation.3 | async-start | bytes 17825792 | tf_op jit(solution)/shard_map/all_gather | solution.py:73
  455.8 17.8 %copy-start.3 = (f32[16,1,128,128]{3,2,1,0:T(8,128)S(1)}, f32[16,1,128,128]{3,2,1,0:T(8,128)}, u32[]{:S(2)}) copy-start(f32[16,1,128,128]{3,2,1,0:T(8,128)} %fusion.28) | copy-start | bytes 3145732
  455.8 40.5 %copy-start.1 = (f32[16,1,128,128]{3,2,1,0:T(8,128)S(1)}, f32[16,1,128,128]{3,2,1,0:T(8,128)}, u32[]{:S(2)}) copy-start(f32[16,1,128,128]{3,2,1,0:T(8,128)} %param.11) | copy-start | bytes 3145732
Sparse Core Ops, SparseCore 0:
  32.6 174.9 all-gather.2
  210.7 110.6 all-gather.4
